TPU v7x, 32 devices: a whole 2x2x4 slice. The times are simulated.
32 devices in a mesh: cfg: 2 (over y), space: 8 (over z, x), tm: 2 (over core).
Axes of the slice: x: 2, y: 2, z: 4, core: 2. Of those that a mesh axis runs over, the one named last changes fastest.
Arguments:
- eigvecs: bfloat16 [4, 2, 3, 1536, 256], P(('cfg', 'tm'), None, None, 'space'), parts along dimension 0, may hold values from -6 to 6
- momenta: int32 [3, 3], replicated, may hold values from -2 to 2, as said below
- pair_list: int32 [8, 2], P('tm'), may hold values from 0 to 1
- panels: bfloat16 [16, 2, 1024, 1024], P(('cfg', 'tm'), None, 'space'), parts along dimension 0, may hold values from -6 to 6
Outputs:
- dressed: bfloat16 [16, 3, 2, 1024, 1024], P(('cfg', 'tm'), None, None, 'space'), parts along dimension 0
There are 2 independent parts, one for each index of `cfg`. A program takes and returns all parts, laid end to end along the dimension named above; an argument that names none is the same for every part. Nothing has to cross between parts.
Inputs may be any that keep to these rules, and one draw needn't show every extreme that they name: `momenta`: the first component of every momentum is nonzero.
All inputs are finite; a program needn't handle non-finite values.
Results may differ from a plain program's by a relative error of at most 0.0075.
Values may be sent and summed in bfloat16 or wider, within the bound.
A program may use at most 64 MiB of HBM per device.

v0:
```python
import math
import jax
import jax.numpy as jnp
from jax import lax
from jax.sharding import PartitionSpec as P

LX = 64


def phased_block(cosine, sine_part, real_part, imag_part):
    cos_col = cosine[:, None]
    sin_col = sine_part[:, None]
    wave_re = cos_col * real_part + sin_col * imag_part
    wave_im = cos_col * imag_part - sin_col * real_part
    upper = jnp.concatenate([wave_re, wave_im], -1)
    lower = jnp.concatenate([wave_im, -wave_re], -1)
    return jnp.stack([upper, lower], -4).astype(jnp.bfloat16)


def local(eigvecs, momenta, pair_list, panels):
    slice_count, _, colors, slab_sites, vectors = eigvecs.shape
    mom_count = momenta.shape[0]
    space_count = lax.axis_size("space")
    first_site = lax.axis_index("space") * slab_sites
    site_index = first_site + jnp.arange(slab_sites, dtype=jnp.int32)
    xpos = site_index % LX
    ypos = site_index // LX % LX
    zpos = site_index // (LX * LX)
    wave = (
        momenta[:, 0:1] * xpos[None, :]
        + momenta[:, 1:2] * ypos[None, :]
        + momenta[:, 2:3] * zpos[None, :]
    )
    wave = jnp.mod(wave, LX)
    angle = wave.astype(jnp.float32) * jnp.float32(2.0 * math.pi / LX)
    cosine = jnp.cos(angle)
    sine_part = jnp.sin(angle)
    factor = 1.0 / math.sqrt(6.0 * slab_sites * space_count * vectors)
    real_part = eigvecs[:, 0].astype(jnp.float32)
    imag_part = eigvecs[:, 1].astype(jnp.float32)
    phased_all = jnp.concatenate(
        [
            phased_block(cosine[moment], sine_part[moment], real_part, imag_part)
            for moment in range(mom_count)
        ],
        -1,
    )
    phased_all = phased_all.reshape(slice_count, 2, colors, slab_sites, mom_count, 2 * vectors)
    gram_local = jnp.einsum(
        "trcsk,trcsml->tmkl", eigvecs, phased_all, preferred_element_type=jnp.float32
    )
    gram_local = factor * gram_local
    summed = lax.psum(gram_local, "space")
    own_fields = summed.astype(jnp.bfloat16)
    meson_fields = lax.all_gather(own_fields, "tm", axis=0, tiled=True)
    pair_count = pair_list.shape[0]
    panel_rows = panels.shape[2]
    panel_width = panels.shape[3]
    spins = panel_width // vectors
    source_fields = jnp.take(meson_fields, pair_list[:, 0], axis=0).reshape(
        pair_count, mom_count, vectors, 2, vectors
    )
    sink_fields = jnp.take(meson_fields, pair_list[:, 1], axis=0).reshape(
        pair_count, mom_count, vectors, 2, vectors
    )
    panel_parts = panels.reshape(pair_count, 2, panel_rows, spins, vectors)
    panel_re = panel_parts[:, 0]
    panel_im = panel_parts[:, 1]
    panel_mix = jnp.stack(
        [jnp.stack([panel_re, panel_im], 1), jnp.stack([panel_im, -panel_re], 1)], 1
    )
    right_dressed = jnp.einsum(
        "porxbk,pmlrk->pmoxbl", panel_mix, source_fields, preferred_element_type=jnp.float32
    )
    right_dressed = right_dressed.astype(jnp.bfloat16).reshape(
        pair_count * mom_count, 2, panel_rows, panel_width
    )
    turned = lax.all_to_all(right_dressed, "space", split_axis=3, concat_axis=2, tiled=True)
    column_count = turned.shape[3]
    turned = turned.reshape(pair_count, mom_count, 2, spins, vectors, column_count)
    turned_re = turned[:, :, 0]
    turned_im = turned[:, :, 1]
    mixed_parts = jnp.stack(
        [jnp.stack([turned_re, -turned_im], 2), jnp.stack([turned_im, turned_re], 2)], 2
    )
    dressed = jnp.einsum(
        "pmorajc,pmkrj->pmocak", mixed_parts, sink_fields, preferred_element_type=jnp.float32
    )
    return dressed.reshape(pair_count, mom_count, 2, column_count, panel_width).astype(jnp.bfloat16)


def solution(mesh):
    placed = (
        P(("cfg", "tm"), None, None, "space", None),
        P(),
        P("tm", None),
        P(("cfg", "tm"), None, "space", None),
    )
    return jax.shard_map(
        local,
        mesh=mesh,
        in_specs=placed,
        out_specs=P(("cfg", "tm"), None, None, "space", None),
        check_vma=False,
    )
```

profile of v0, /device:TPU:0, one launch (start us, length us, event | category | flops | bytes accessed | tf_op | source)
XLA Modules:
  0.0 343.8 jit_solution(5193341892418195743)
XLA Ops:
  7.8 1.6 fusion.30
  11.3 83.3 %all-reduce.1 = bf16[1,3,256,512]{2,3,1,0:T(8,128)(2,1)S(1)} all-reduce(f32[1,3,256,512]{2,3,1,0:T(8,128)S(1)} %fusion.17), channel_id=1, replica_groups=mesh['cfg'=2,'space'=8,'tm'=2] {'space'}, use_global_device_ids=true, to_apply=%region_0.1 | all-reduce | flops 393216 | bytes 2359296 | tf_op jit(solution)/shard_map/psum | solution.py:53
  94.7 1.3 copy.48
  95.9 3.0 copy.49
  99.0 1.5 fusion.42
  100.4 1.5 copy.77
  103.2 2.4 copy.76
  105.6 2.3 copy.53
  107.9 2.7 maximum_bitcast_fusion.6
  110.7 2.2 gather_fusion.1
  112.8 2.0 broadcast_select_fusion
  114.9 3.8 %reshape.415 = bf16[4,3,256,2,256]{4,3,2,1,0:T(2,128)(2,1)S(1)} reshape(bf16[4,3,256,512]{3,2,1,0:T(8,128)(2,1)} %broadcast_select_fusion) | data formatting | bytes 6291456 | tf_op jit(solution)/shard_map/reshape | solution.py:60
  118.6 6.2 %bitcast_convert_fusion.1 = bf16[4,3,256,2,128,4]{4,2,5,3,1,0:T(8,128)(2,1)S(1)} fusion(bf16[4,1,2,128,4,256]{5,3,2,4,1,0:T(8,128)(2,1)} %maximum_bitcast_fusion.6, bf16[4,1,2,128,4,256]{5,3,2,4,1,0:T(8,128)(2,1)} %copy.53, bf16[4,3,256,2,256,1,1]{4,3,2,1,0,6,5:T(2,128)(2,1)S(1)} %bitcast.120), kind=kOutput, calls=%fused_computation.7 | convolution fusion | flops 3232759808 | bytes 13631488 | tf_op jit(solution)/shard_map/porxbk,pmlrk->pmoxbl/dot_general | solution.py:72
  124.8 36.6 %copy.55 = bf16[12,2,128,1024]{2,1,0,3:T(2,128)(2,1)} copy(bf16[12,2,128,1024]{2,3,1,0:T(8,128)(2,1)S(1)} %bitcast.117) | data formatting | bytes 12582912 | tf_op jit(solution)/shard_map/reshape | solution.py:75
  161.5 5.1 %all-to-all-start = ((bf16[12,2,128,1024]{2,1,0,3:T(2,128)(2,1)}), bf16[12,2,128,1024]{2,1,0,3:T(2,128)(2,1)}, u32[]{:S(2)}, u32[]{:S(2)}) async-start(bf16[12,2,128,1024]{2,1,0,3:T(2,128)(2,1)} %copy.55), calls=%async_computation | async-start | bytes 12582912 | tf_op jit(solution)/shard_map/all_to_all | solution.py:78
  166.6 2.5 gather_fusion
  169.0 2.3 broadcast_select_fusion.1
  171.3 3.1 reshape.414
  174.3 125.2 %all-to-all-done = bf16[12,2,128,1024]{2,1,0,3:T(2,128)(2,1)} async-done(((bf16[12,2,128,1024]{2,1,0,3:T(2,128)(2,1)}), bf16[12,2,128,1024]{2,1,0,3:T(2,128)(2,1)}, u32[]{:S(2)}, u32[]{:S(2)}) %all-to-all-start) | async-done | bytes 6291488 | tf_op jit(solution)/shard_map/all_to_all | solution.py:78
  299.6 6.9 %copy.56 = bf16[12,2,128,1024]{2,3,1,0:T(8,128)(2,1)} copy(bf16[12,2,128,1024]{2,1,0,3:T(2,128)(2,1)} %all-to-all-done) | data formatting | bytes 12582912 | tf_op jit(solution)/shard_map/all_to_all | solution.py:78
  306.4 8.6 %copy.57 = bf16[12,2,8,128,128]{4,3,2,1,0:T(8,128)(2,1)} copy(bf16[12,2,8,128,128]{3,4,2,1,0:T(8,128)(2,1)} %bitcast.114) | data formatting | bytes 12582912 | tf_op jit(solution)/shard_map/all_to_all | solution.py:78
  315.1 3.4 slice_bitcast_fusion
  321.1 7.2 %bitcast_convert_fusion = bf16[4,3,256,2,4,128]{5,2,4,3,1,0:T(8,128)(2,1)} fusion(bf16[4,3,1,2,4,256,128]{6,5,3,4,2,1,0:T(8,128)(2,1)S(1)} %get-tuple-element.16, bf16[4,3,1,2,4,256,128]{6,5,3,4,2,1,0:T(8,128)(2,1)S(1)} %get-tuple-element.15, bf16[4,3,256,2,256,1,1]{4,3,2,1,0,6,5:T(2,128)(2,1)} %bitcast.119), kind=kOutput, calls=%fused_computation.6 | convolution fusion | flops 3249537024 | bytes 22020096 | tf_op jit(solution)/shard_map/pmorajc,pmkrj->pmocak/dot_general | solution.py:86
  328.3 8.6 %copy.62 = bf16[4,3,2,128,1024]{4,3,2,1,0:T(8,128)(2,1)} copy(bf16[4,3,2,128,1024]{3,4,2,1,0:T(8,128)(2,1)} %bitcast.118) | data formatting | bytes 12582912 | tf_op jit(solution)/shard_map/convert_element_type | solution.py:89
  (30 shorter events, 7.0 us)
Async XLA Ops:
  6.5 104.1 %all-gather.2.cloned.1.call-start = ((), (), s32[]{:S(2)}) async-start(), calls=%async_computation.1 | async-start | bytes 2359296 | tf_op jit(solution)/shard_map/all_gather | solution.py:55
  7.7 1.8 copy-start.3
  103.2 4.7 %copy-start.4 = (s32[4,2]{0,1:T(2,128)S(1)}, s32[4,2]{0,1:T(2,128)}, u32[]{:S(2)}) copy-start(s32[4,2]{0,1:T(2,128)} %param.8) | copy-start | bytes 100
  103.2 4.7 %copy-start.2 = (bf16[4,1,128,4,256]{4,2,1,3,0:T(8,128)(2,1)S(1)}, bf16[4,1,128,4,256]{4,2,1,3,0:T(8,128)(2,1)}, u32[]{:S(2)}) copy-start(bf16[4,1,128,4,256]{4,2,1,3,0:T(8,128)(2,1)} %neg.44) | copy-start | bytes 3145732
  161.5 5.1 %copy-start.1 = (bf16[2,3,256,512]{3,2,1,0:T(8,128)(2,1)S(1)}, bf16[2,3,256,512]{3,2,1,0:T(8,128)(2,1)}, u32[]{:S(2)}) copy-start(bf16[2,3,256,512]{3,2,1,0:T(8,128)(2,1)} %all-gather.2.cloned.1.call-done) | copy-start | bytes 4718596
  161.5 138.1 %all-to-all-start = ((bf16[12,2,128,1024]{2,1,0,3:T(2,128)(2,1)}), bf16[12,2,128,1024]{2,1,0,3:T(2,128)(2,1)}, u32[]{:S(2)}, u32[]{:S(2)}) async-start(bf16[12,2,128,1024]{2,1,0,3:T(2,128)(2,1)} %copy.55), calls=%async_computation | async-start | bytes 12582912 | tf_op jit(solution)/shard_map/all_to_all | solution.py:78
  315.1 4.6 %copy-start = (bf16[12,2,8,128,128]{4,3,2,1,0:T(8,128)(2,1)S(1)}, bf16[12,2,8,128,128]{4,3,2,1,0:T(8,128)(2,1)}, u32[]{:S(2)}) copy-start(bf16[12,2,8,128,128]{4,3,2,1,0:T(8,128)(2,1)} %copy.57) | copy-start | bytes 18874372
Sparse Core Ops, SparseCore 0:
  96.1 7.9 all-gather.1
where the time goes:
time: 345 us; the launch traced here: 344 us
  waiting for transfers between devices  125 us (36%)
  local copies, waits for them, and re-layouts  89.8 us (26%)
  blocking collectives  83.3 us (24%)
  matrix products  14.6 us (4%)
  between operations  13.6 us (4%)
  other arithmetic  12 us (3%)
  starting transfers between devices  5.08 us (1%)
    all_to_all x1, waiting for transfers between devices, local(): lax.all_to_all(right_dressed, 'space', split_axis=3, concat_axis=2, tiled...  125 us
    psum x1, blocking collectives, local(): summed = lax.psum(gram_local, 'space')  83.3 us
    reshape x1, local copies, waits for them, and re-layouts, local(): right_dressed.astype(jnp.bfloat16)  36.6 us
    all_to_all x2, local copies, waits for them, and re-layouts, local(): lax.all_to_all(right_dressed, 'space', split_axis=3, concat_axis=2, tiled...  15.5 us
    unnamed x14, local copies, waits for them, and re-layouts  11.6 us
    convert_element_type x1, local copies, waits for them, and re-layouts, local(): dressed.reshape(pair_count, mom_count, 2, column_count, panel_width)  8.62 us
    dot_general x1, matrix products, local(): jnp.einsum('pmorajc,pmkrj->pmocak', mixed_parts, sink_fields, preferred_e...  7.2 us
  transfers between devices with their start and end apart: 2, of which 1 were waited for; matrix products, arithmetic and copies ran while one was open for 7% of the time, Pallas kernels for 0%

commit v1 on v0

--- a/solution.py
+++ b/solution.py
@@ -5,6 +5,14 @@
 from jax.sharding import PartitionSpec as P
 
 LX = 64
+
+
+def added_up(x, mesh_axis):
+    size, total = (lax.axis_size(mesh_axis), x)
+    for stride in [1 << k for k in range(size.bit_length() - 1)]:
+        route = [(i, i ^ stride) for i in range(size)]
+        total = total + lax.ppermute(total, mesh_axis, route)
+    return total
 
 
 def phased_block(cosine, sine_part, real_part, imag_part):
@@ -50,7 +58,7 @@
         "trcsk,trcsml->tmkl", eigvecs, phased_all, preferred_element_type=jnp.float32
     )
     gram_local = factor * gram_local
-    summed = lax.psum(gram_local, "space")
+    summed = added_up(gram_local, "space")
     own_fields = summed.astype(jnp.bfloat16)
     meson_fields = lax.all_gather(own_fields, "tm", axis=0, tiled=True)
     pair_count = pair_list.shape[0]

time: 345 us -> 410 us (1.19)
  waiting for transfers between devices: 125 us -> 266 us
  blocking collectives: 83.3 us -> 0 us
  starting transfers between devices: 5.08 us -> 13 us
    ppermute x0 -> x3, waiting for transfers between devices: none -> 135 us  [added_up(): total = total + lax.ppermute(total, mesh_axis, route)]
    psum x1 -> x0, blocking collectives: 83.3 us -> none  [local(): summed = lax.psum(gram_local, 'space')]
    ppermute x0 -> x3, starting transfers between devices: none -> 7.54 us  [added_up(): total = total + lax.ppermute(total, mesh_axis, route)]
    all_to_all x1, waiting for transfers between devices: 125 us -> 131 us  [local(): lax.all_to_all(right_dressed, 'space', split_axis=3, concat_axis=2, tiled...]
  transfers between devices with their start and end apart: 2 -> 5, of which waited for: 1 -> 4; matrix products, arithmetic and copies ran while one was open for 7% -> 6% of each run, Pallas kernels for 0% -> 0%
where the time goes in v1:
time: 410 us; the launch traced here: 409 us
  waiting for transfers between devices  266 us (65%)
  local copies, waits for them, and re-layouts  89.9 us (22%)
  matrix products  14.6 us (4%)
  between operations  13.6 us (3%)
  starting transfers between devices  13 us (3%)
  other arithmetic  12.7 us (3%)
    ppermute x3, waiting for transfers between devices, added_up(): total = total + lax.ppermute(total, mesh_axis, route)  135 us
    all_to_all x1, waiting for transfers between devices, local(): lax.all_to_all(right_dressed, 'space', split_axis=3, concat_axis=2, tiled...  131 us
    reshape x1, local copies, waits for them, and re-layouts, local(): right_dressed.astype(jnp.bfloat16)  36.6 us
    all_to_all x2, local copies, waits for them, and re-layouts, local(): lax.all_to_all(right_dressed, 'space', split_axis=3, concat_axis=2, tiled...  15.6 us
    unnamed x14, local copies, waits for them, and re-layouts  11.6 us
    convert_element_type x1, local copies, waits for them, and re-layouts, local(): dressed.reshape(pair_count, mom_count, 2, column_count, panel_width)  8.62 us
  transfers between devices with their start and end apart: 5, of which 4 were waited for; matrix products, arithmetic and copies ran while one was open for 6% of the time, Pallas kernels for 0%

profile of v1, /device:TPU:0, one launch (start us, length us, event | category | flops | bytes accessed | tf_op | source)
XLA Modules:
  0.0 409.4 jit_solution(398115430253767199)
XLA Ops:
  11.3 3.0 collective-permute-start
  14.3 34.4 %collective-permute-done = f32[1,3,256,512]{2,3,1,0:T(8,128)S(1)} collective-permute-done((f32[1,3,256,512]{2,3,1,0:T(8,128)S(1)}, f32[1,3,256,512]{2,3,1,0:T(8,128)S(1)}, u32[]{:S(2)}, u32[]{:S(2)}) %collective-permute-start) | collective-permute-done | bytes 1572896 | tf_op jit(solution)/shard_map/ppermute | solution.py:14
  50.8 33.7 %collective-permute-done.1 = f32[1,3,256,512]{2,3,1,0:T(8,128)S(1)} collective-permute-done((f32[1,3,256,512]{2,3,1,0:T(8,128)S(1)}, f32[1,3,256,512]{2,3,1,0:T(8,128)S(1)}, u32[]{:S(2)}, u32[]{:S(2)}) %collective-permute-start.1) | collective-permute-done | bytes 1572896 | tf_op jit(solution)/shard_map/ppermute | solution.py:14
  84.8 2.6 collective-permute-start.2
  87.4 66.8 %collective-permute-done.2 = f32[1,3,256,512]{2,3,1,0:T(8,128)S(1)} collective-permute-done((f32[1,3,256,512]{2,3,1,0:T(8,128)S(1)}, f32[1,3,256,512]{2,3,1,0:T(8,128)S(1)}, u32[]{:S(2)}, u32[]{:S(2)}) %collective-permute-start.2) | collective-permute-done | bytes 1572896 | tf_op jit(solution)/shard_map/ppermute | solution.py:14
  155.7 3.0 copy.49
  162.9 2.4 copy.76
  165.3 2.4 copy.53
  167.8 2.7 maximum_bitcast_fusion.6
  170.5 2.2 gather_fusion.1
  172.7 2.0 broadcast_select_fusion
  174.7 3.8 reshape.415
  178.5 6.2 %bitcast_convert_fusion.1 = bf16[4,3,256,2,128,4]{4,2,5,3,1,0:T(8,128)(2,1)S(1)} fusion(bf16[4,1,2,128,4,256]{5,3,2,4,1,0:T(8,128)(2,1)} %maximum_bitcast_fusion.6, bf16[4,1,2,128,4,256]{5,3,2,4,1,0:T(8,128)(2,1)} %copy.53, bf16[4,3,256,2,256,1,1]{4,3,2,1,0,6,5:T(2,128)(2,1)S(1)} %bitcast.120), kind=kOutput, calls=%fused_computation.7 | convolution fusion | flops 3232759808 | bytes 13631488 | tf_op jit(solution)/shard_map/porxbk,pmlrk->pmoxbl/dot_general | solution.py:80
  184.7 36.6 %copy.55 = bf16[12,2,128,1024]{2,1,0,3:T(2,128)(2,1)} copy(bf16[12,2,128,1024]{2,3,1,0:T(8,128)(2,1)S(1)} %bitcast.117) | data formatting | bytes 12582912 | tf_op jit(solution)/shard_map/reshape | solution.py:83
  221.3 5.5 %all-to-all-start = ((bf16[12,2,128,1024]{2,1,0,3:T(2,128)(2,1)}), bf16[12,2,128,1024]{2,1,0,3:T(2,128)(2,1)}, u32[]{:S(2)}, u32[]{:S(2)}) async-start(bf16[12,2,128,1024]{2,1,0,3:T(2,128)(2,1)} %copy.55), calls=%async_computation | async-start | bytes 12582912 | tf_op jit(solution)/shard_map/all_to_all | solution.py:86
  226.8 2.5 gather_fusion
  229.2 2.3 broadcast_select_fusion.1
  231.5 3.1 reshape.414
  234.6 130.6 %all-to-all-done = bf16[12,2,128,1024]{2,1,0,3:T(2,128)(2,1)} async-done(((bf16[12,2,128,1024]{2,1,0,3:T(2,128)(2,1)}), bf16[12,2,128,1024]{2,1,0,3:T(2,128)(2,1)}, u32[]{:S(2)}, u32[]{:S(2)}) %all-to-all-start) | async-done | bytes 6291488 | tf_op jit(solution)/shard_map/all_to_all | solution.py:86
  365.2 6.9 %copy.56 = bf16[12,2,128,1024]{2,3,1,0:T(8,128)(2,1)} copy(bf16[12,2,128,1024]{2,1,0,3:T(2,128)(2,1)} %all-to-all-done) | data formatting | bytes 12582912 | tf_op jit(solution)/shard_map/all_to_all | solution.py:86
  372.1 8.7 %copy.57 = bf16[12,2,8,128,128]{4,3,2,1,0:T(8,128)(2,1)} copy(bf16[12,2,8,128,128]{3,4,2,1,0:T(8,128)(2,1)} %bitcast.114) | data formatting | bytes 12582912 | tf_op jit(solution)/shard_map/all_to_all | solution.py:86
  380.8 3.4 slice_bitcast_fusion
  386.8 7.2 %bitcast_convert_fusion = bf16[4,3,256,2,4,128]{5,2,4,3,1,0:T(8,128)(2,1)} fusion(bf16[4,3,1,2,4,256,128]{6,5,3,4,2,1,0:T(8,128)(2,1)S(1)} %get-tuple-element.16, bf16[4,3,1,2,4,256,128]{6,5,3,4,2,1,0:T(8,128)(2,1)S(1)} %get-tuple-element.15, bf16[4,3,256,2,256,1,1]{4,3,2,1,0,6,5:T(2,128)(2,1)} %bitcast.119), kind=kOutput, calls=%fused_computation.6 | convolution fusion | flops 3249537024 | bytes 22020096 | tf_op jit(solution)/shard_map/pmorajc,pmkrj->pmocak/dot_general | solution.py:94
  393.9 8.6 %copy.62 = bf16[4,3,2,128,1024]{4,3,2,1,0:T(8,128)(2,1)} copy(bf16[4,3,2,128,1024]{3,4,2,1,0:T(8,128)(2,1)} %bitcast.118) | data formatting | bytes 12582912 | tf_op jit(solution)/shard_map/convert_element_type | solution.py:97
  (38 shorter events, 15.3 us)
Async XLA Ops:
  6.5 164.0 %all-gather.2.cloned.1.call-start = ((), (), s32[]{:S(2)}) async-start(), calls=%async_computation.1 | async-start | bytes 2359296 | tf_op jit(solution)/shard_map/all_gather | solution.py:63
  7.7 1.8 copy-start.3
  11.3 37.4 %collective-permute-start = (f32[1,3,256,512]{2,3,1,0:T(8,128)S(1)}, f32[1,3,256,512]{2,3,1,0:T(8,128)S(1)}, u32[]{:S(2)}, u32[]{:S(2)}) collective-permute-start(f32[1,3,256,512]{2,3,1,0:T(8,128)S(1)} %fusion.17), channel_id=1, source_target_pairs={{0,2},{2,0},{4,6},{6,4},{8,10},{10,8},{12,14},{14,12},{1,3},{3,1},... | collective-permute-start | bytes 4718600 | tf_op jit(solution)/shard_map/ppermute | solution.py:14
  48.9 35.6 %collective-permute-start.1 = (f32[1,3,256,512]{2,3,1,0:T(8,128)S(1)}, f32[1,3,256,512]{2,3,1,0:T(8,128)S(1)}, u32[]{:S(2)}, u32[]{:S(2)}) collective-permute-start(f32[1,3,256,512]{2,3,1,0:T(8,128)S(1)} %add.123), channel_id=1, source_target_pairs={{0,4},{2,6},{4,0},{6,2},{8,12},{10,14},{12,8},{14,10},{1,5},{3,7},... | collective-permute-start | bytes 4718600 | tf_op jit(solution)/shard_map/ppermute | solution.py:14
  84.8 69.4 %collective-permute-start.2 = (f32[1,3,256,512]{2,3,1,0:T(8,128)S(1)}, f32[1,3,256,512]{2,3,1,0:T(8,128)S(1)}, u32[]{:S(2)}, u32[]{:S(2)}) collective-permute-start(f32[1,3,256,512]{2,3,1,0:T(8,128)S(1)} %add.124), channel_id=1, source_target_pairs={{0,8},{2,10},{4,12},{6,14},{8,0},{10,2},{12,4},{14,6},{1,9},{3,11}... | collective-permute-start | bytes 4718600 | tf_op jit(solution)/shard_map/ppermute | solution.py:14
  162.9 4.8 %copy-start.4 = (s32[4,2]{0,1:T(2,128)S(1)}, s32[4,2]{0,1:T(2,128)}, u32[]{:S(2)}) copy-start(s32[4,2]{0,1:T(2,128)} %param.8) | copy-start | bytes 100
  162.9 4.8 %copy-start.2 = (bf16[4,1,128,4,256]{4,2,1,3,0:T(8,128)(2,1)S(1)}, bf16[4,1,128,4,256]{4,2,1,3,0:T(8,128)(2,1)}, u32[]{:S(2)}) copy-start(bf16[4,1,128,4,256]{4,2,1,3,0:T(8,128)(2,1)} %neg.44) | copy-start | bytes 3145732
  221.3 5.5 %copy-start.1 = (bf16[2,3,256,512]{3,2,1,0:T(8,128)(2,1)S(1)}, bf16[2,3,256,512]{3,2,1,0:T(8,128)(2,1)}, u32[]{:S(2)}) copy-start(bf16[2,3,256,512]{3,2,1,0:T(8,128)(2,1)} %all-gather.2.cloned.1.call-done) | copy-start | bytes 4718596
  221.3 143.9 %all-to-all-start = ((bf16[12,2,128,1024]{2,1,0,3:T(2,128)(2,1)}), bf16[12,2,128,1024]{2,1,0,3:T(2,128)(2,1)}, u32[]{:S(2)}, u32[]{:S(2)}) async-start(bf16[12,2,128,1024]{2,1,0,3:T(2,128)(2,1)} %copy.55), calls=%async_computation | async-start | bytes 12582912 | tf_op jit(solution)/shard_map/all_to_all | solution.py:86
  380.8 4.6 %copy-start = (bf16[12,2,8,128,128]{4,3,2,1,0:T(8,128)(2,1)S(1)}, bf16[12,2,8,128,128]{4,3,2,1,0:T(8,128)(2,1)}, u32[]{:S(2)}) copy-start(bf16[12,2,8,128,128]{4,3,2,1,0:T(8,128)(2,1)} %copy.57) | copy-start | bytes 18874372
Sparse Core Ops, SparseCore 0:
  155.8 10.6 all-gather.1
